TPU v7x, 128 devices: a whole 4x4x4 slice. The times are simulated.
128 devices in a mesh: freq: 4 (over z_lo, core), facet: 32 (over y, x, z_hi).
Axes of the slice: x: 4, y: 4, z: 4 (z_hi: 2, z_lo: 2; z = z_hi * 2 + z_lo), core: 2. Of those that a mesh axis runs over, the one named last changes fastest.
Arguments:
- visibilities: float32 [64, 2, 2048], P('facet', None, 'freq'), may hold values from -6 to 6
- weights: float32 [64, 2048], P('facet', 'freq'), may hold values from 0.1 to 1
- uv_cells: int32 [64, 2, 2048], P('facet', None, 'freq'), may hold values from -16384 to 16383
- flags: int32 [64, 2048], P('facet', 'freq'), may hold values from 0 to 1, as said below
- plan: int32 [64], replicated, may hold values from 0 to 63, each once
- beam: float32 [32, 64], P('facet'), may hold values from 0.2 to 1
- facets: int32 [32, 2], P('facet'), may hold values from 0 to 255
Outputs:
- dirty_image: float32 [32, 128, 128], P('facet', 'freq')
Inputs may be any that keep to these rules, and one draw needn't show every extreme that they name: `flags`: in each block, each frequency group's 512 rows hold at most 256 unflagged rows; in every draw some block holds exactly 256 in every group. `plan`: each of the 64 blocks is read at exactly one step.
All inputs are finite; a program needn't handle non-finite values.
Results may differ from a plain program's by a relative error of at most 0.0037.
Values sent between devices are 32-bit elements; how exact they have to be, the bound alone decides.
No kernel may reach another device: no remote copies, remote signals or barrier semaphores. Data moves between devices by JAX's collectives and lax.ppermute only.
A program may use at most 64 MiB of HBM per device.

v0:
```python
import math
import jax
import jax.numpy as jnp
from jax import lax
from jax.sharding import PartitionSpec as P

P_SIZE = 128
IMG = 32768
full_turn = 2.0 * math.pi
slab_limit = 16384
fine_count = 16


def angle_table(factors, cells):
    turns = jnp.mod(factors[:, None] * cells[None, :], IMG).astype(jnp.float32) * (full_turn / IMG)
    return (jnp.cos(turns), jnp.sin(turns))


def phase_table(base, cells):
    coarse_count = P_SIZE // fine_count
    base_cos, base_sin = angle_table(jnp.reshape(base, (1,)), cells)
    coarse_cos, coarse_sin = angle_table(
        jnp.arange(coarse_count, dtype=jnp.int32) * fine_count, cells
    )
    fine_cos, fine_sin = angle_table(jnp.arange(fine_count, dtype=jnp.int32), cells)
    outer_cos = base_cos * coarse_cos - base_sin * coarse_sin
    outer_sin = base_sin * coarse_cos + base_cos * coarse_sin
    full_cos = (
        outer_cos[:, None, :] * fine_cos[None, :, :] - outer_sin[:, None, :] * fine_sin[None, :, :]
    )
    full_sin = (
        outer_sin[:, None, :] * fine_cos[None, :, :] + outer_cos[:, None, :] * fine_sin[None, :, :]
    )
    extent = cells.shape[0]
    return (full_cos.reshape(P_SIZE, extent), full_sin.reshape(P_SIZE, extent))


def facet_image(samples, facet_col, facet_row):
    u_cells = samples[3].astype(jnp.int32)
    v_cells = samples[4].astype(jnp.int32)
    cos_u, sin_u = phase_table(facet_col * P_SIZE - IMG // 2, u_cells)
    real_part = samples[0] * samples[2]
    imag_part = samples[1] * samples[2]
    left = jnp.concatenate(
        [real_part * cos_u - imag_part * sin_u, -(real_part * sin_u + imag_part * cos_u)], axis=1
    ).astype(jnp.bfloat16)
    cos_v, sin_v = phase_table(facet_row * P_SIZE - IMG // 2, v_cells)
    right = jnp.concatenate([cos_v, sin_v], axis=1).astype(jnp.bfloat16)
    return lax.dot_general(
        left, right, (((1,), (1,)), ((), ())), preferred_element_type=jnp.float32
    )


def slab_image(samples, facet_col, facet_row):
    extent = samples.shape[1]
    slabs = samples.reshape(5, extent // slab_limit, slab_limit).transpose(1, 0, 2)

    def advance(running, slab):
        return (running + facet_image(slab, facet_col, facet_row), None)

    summed, _ = lax.scan(advance, jnp.zeros((P_SIZE, P_SIZE), jnp.float32), slabs)
    return summed


def flatten_blocks(packed, factors):
    scaled = packed[:, 2, :] * factors[:, None]
    joined = jnp.concatenate([packed[:, :2, :], scaled[:, None, :], packed[:, 3:, :]], axis=1)
    return joined.transpose(1, 0, 2).reshape(5, -1)


def body(visibilities, weights, uv_cells, flags, plan, beam, facets):
    live = weights * flags.astype(jnp.float32)
    packed = jnp.concatenate([visibilities, live[:, None, :], uv_cells.astype(jnp.float32)], axis=1)
    total_blocks = plan.shape[0]
    matches = (plan[:, None] == jnp.arange(total_blocks, dtype=jnp.int32)[None, :]).astype(
        jnp.float32
    )
    gains = jnp.sum(beam[0][:, None] * matches, axis=0)
    facet_col = facets[0, 0]
    facet_row = facets[0, 1]
    image = slab_image(
        flatten_blocks(lax.all_gather(packed, "facet", axis=0, tiled=True), gains),
        facet_col,
        facet_row,
    )
    share = lax.psum_scatter(image, "freq", scatter_dimension=0, tiled=True)
    scale = 2.0 / math.sqrt(total_blocks * weights.shape[1] * lax.axis_size("freq"))
    return (share * scale)[None]


def solution(mesh):
    in_specs = (
        P("facet", None, "freq"),
        P("facet", "freq"),
        P("facet", None, "freq"),
        P("facet", "freq"),
        P(),
        P("facet", None),
        P("facet", None),
    )
    out_specs = P("facet", "freq", None)
    return jax.shard_map(body, mesh=mesh, in_specs=in_specs, out_specs=out_specs, check_vma=False)
```

profile of v0, /device:TPU:1, one launch (start us, length us, event | category | flops | bytes accessed | tf_op | source)
XLA Modules:
  0.0 203.0 jit_solution(12933893324455298943)
XLA Ops:
  6.5 0.7 convert_multiply_fusion
  7.3 0.7 convert_element_type.174
  8.0 0.7 pad_maximum_fusion.1
  8.7 88.1 %all_gather.3 = f32[64,5,512]{2,1,0:T(8,128)S(1)} all-gather(f32[2,5,512]{2,1,0:T(8,128)S(1)} %pad_maximum_fusion.1), channel_id=1, replica_groups=mesh['freq'=4,'facet'=32] {'facet'}, dimensions={0}, use_global_device_ids=true | all-gather | bytes 675840 | tf_op jit(solution)/shard_map/all_gather | solution.py:82
  96.9 0.8 select_reduce_fusion
  97.9 1.3 fusion.55
  100.8 67.1 %while.14 = (s32[]{:T(128)}, f32[128,128]{1,0:T(8,128)S(1)}, f32[2,5,16384]{2,1,0:T(8,128)S(1)}, s32[]{:T(128)}, s32[]{:T(128)}, /*index=5*/s32[]{:T(128)}, s32[]{:T(128)}, s32[]{}, s32[]{}, s32[]{}, /*index=10*/s32[]{}) while((s32[]{:T(128)}, f32[128,128]{1,0:T(8,128)S(1)}, f32[2,5,16384]{2,1,0:T(8,128)S(1)}, s32[]{:T(128)}, ...), condition=%wide.region_2.3_spmd.clone, body=%wide.region_1.2_spmd.clone.sunk | while | flops 1168670720 | bytes 81461504 | solution.py:61
  101.7 4.3 %multiply_subtract_fusion.5 = (f32[8,16384]{1,0:T(8,128)S(1)}, f32[8,16384]{1,0:T(8,128)S(1)}, f32[8,16384]{1,0:T(8,128)S(1)}, f32[8,16384]{1,0:T(8,128)S(1)}) fusion(f32[16384]{0:T(1024)S(1)} %get-tuple-element.221, s32[16384]{0:T(1024)S(1)} %bitcast.58, s32[8]{0:T(128)S(1)} %iota_multiply_fusion.2, f32[16384]{0:T(1024)S(1)} %get-tuple-element.222, ...), kind=kLoop, calls=%fused_computation.62.clone.1 | loop fusion | flops 5242880 | bytes 2490400 | tf_op jit(solution)/shard_map/while/body/eval_jaxpr/sub | solution.py:26
  106.0 4.1 %fusion.67 = (f32[16,16384]{1,0:T(8,128)S(1)}, f32[16,16384]{1,0:T(8,128)S(1)}) fusion(s32[16384]{0:T(1024)S(1)} %bitcast.59), kind=kLoop, calls=%fused_computation.61.clone.1 | loop fusion | flops 3670016 | bytes 2162688 | tf_op jit(solution)/shard_map/while/body/eval_jaxpr/cos | solution.py:16
  110.1 2.3 %multiply_subtract_fusion.6 = (f32[8,16,16384]{2,1,0:T(8,128)S(1)}, f32[8,16,16384]{2,1,0:T(8,128)S(1)}) fusion(f32[16,16384]{1,0:T(8,128)S(1)} %get-tuple-element.230, f32[8,16384]{1,0:T(8,128)S(1)} %get-tuple-element.231, f32[16,16384]{1,0:T(8,128)S(1)} %get-tuple-element.232, f32[8,16384]{1,0:T(8,128)S(1)} %get-tuple-element.233), kind=kLoop, calls=%fused_computation.19.clone.1 | loop fusion | flops 12582912 | bytes 19922944 | tf_op jit(solution)/shard_map/while/body/eval_jaxpr/sub | solution.py:29
  112.4 5.4 %fusion.68 = (bf16[128,16384]{1,0:T(8,128)(2,1)}, bf16[128,16384]{1,0:T(8,128)(2,1)}) fusion(f32[8,16,16384]{2,1,0:T(8,128)S(1)} %get-tuple-element.234, f32[8,16,16384]{2,1,0:T(8,128)S(1)} %get-tuple-element.235, f32[16384]{0:T(1024)S(1)} %bitcast.62, f32[16384]{0:T(1024)S(1)} %bitcast.61), kind=kLoop, calls=%fused_computation.10.clone.1 | loop fusion | flops 18874368 | bytes 25296896 | tf_op jit(solution)/shard_map/convert.4
  117.8 4.1 %fusion.65 = (f32[16,16384]{1,0:T(8,128)S(1)}, f32[16,16384]{1,0:T(8,128)S(1)}) fusion(s32[16384]{0:T(1024)S(1)} %bitcast.56), kind=kLoop, calls=%fused_computation.59.clone.1 | loop fusion | flops 3670016 | bytes 2162688 | tf_op jit(solution)/shard_map/while/body/eval_jaxpr/cos | solution.py:16
  121.9 4.2 %subtract_convert_fusion.2 = (bf16[8,16,16384]{2,1,0:T(8,128)(2,1)}, bf16[8,16,16384]{2,1,0:T(8,128)(2,1)}) fusion(f32[16,16384]{1,0:T(8,128)S(1)} %get-tuple-element.219, f32[8,16384]{1,0:T(8,128)S(1)} %get-tuple-element.225, f32[16,16384]{1,0:T(8,128)S(1)} %get-tuple-element.226, f32[8,16384]{1,0:T(8,128)S(1)} %get-tuple-element.227), kind=kLoop, calls=%fused_computation.17.clone.1 | loop fusion | flops 16777216 | bytes 11534336 | tf_op jit(solution)/shard_map/convert.3
  126.1 8.2 %fusion.69 = f32[128,128]{1,0:T(8,128)S(1)} fusion(bf16[128,16384]{1,0:T(8,128)(2,1)} %bitcast.53, bf16[128,16384]{1,0:T(8,128)(2,1)} %bitcast.52, bf16[128,16384]{1,0:T(8,128)(2,1)} %get-tuple-element.238, bf16[128,16384]{1,0:T(8,128)(2,1)} %get-tuple-element.239, f32[128,128]{1,0:T(8,128)S(1)} %get-tuple-element.252, pred[]{:T(512)S(6)} %compare.15), kind=kOutput, calls=%fused_computation.48.clone.1 | convolution fusion | flops 1107329024 | bytes 16908288 | tf_op jit(solution)/shard_map/while/body/eval_jaxpr/dot_general | solution.py:49
  135.2 4.3 %multiply_subtract_fusion.5 = (f32[8,16384]{1,0:T(8,128)S(1)}, f32[8,16384]{1,0:T(8,128)S(1)}, f32[8,16384]{1,0:T(8,128)S(1)}, f32[8,16384]{1,0:T(8,128)S(1)}) fusion(f32[16384]{0:T(1024)S(1)} %get-tuple-element.221, s32[16384]{0:T(1024)S(1)} %bitcast.58, s32[8]{0:T(128)S(1)} %iota_multiply_fusion.2, f32[16384]{0:T(1024)S(1)} %get-tuple-element.222, ...), kind=kLoop, calls=%fused_computation.62.clone.1 | loop fusion | flops 5242880 | bytes 2490400 | tf_op jit(solution)/shard_map/while/body/eval_jaxpr/sub | solution.py:26
  139.5 4.1 %fusion.67 = (f32[16,16384]{1,0:T(8,128)S(1)}, f32[16,16384]{1,0:T(8,128)S(1)}) fusion(s32[16384]{0:T(1024)S(1)} %bitcast.59), kind=kLoop, calls=%fused_computation.61.clone.1 | loop fusion | flops 3670016 | bytes 2162688 | tf_op jit(solution)/shard_map/while/body/eval_jaxpr/cos | solution.py:16
  143.6 2.3 %multiply_subtract_fusion.6 = (f32[8,16,16384]{2,1,0:T(8,128)S(1)}, f32[8,16,16384]{2,1,0:T(8,128)S(1)}) fusion(f32[16,16384]{1,0:T(8,128)S(1)} %get-tuple-element.230, f32[8,16384]{1,0:T(8,128)S(1)} %get-tuple-element.231, f32[16,16384]{1,0:T(8,128)S(1)} %get-tuple-element.232, f32[8,16384]{1,0:T(8,128)S(1)} %get-tuple-element.233), kind=kLoop, calls=%fused_computation.19.clone.1 | loop fusion | flops 12582912 | bytes 19922944 | tf_op jit(solution)/shard_map/while/body/eval_jaxpr/sub | solution.py:29
  145.9 5.4 %fusion.68 = (bf16[128,16384]{1,0:T(8,128)(2,1)}, bf16[128,16384]{1,0:T(8,128)(2,1)}) fusion(f32[8,16,16384]{2,1,0:T(8,128)S(1)} %get-tuple-element.234, f32[8,16,16384]{2,1,0:T(8,128)S(1)} %get-tuple-element.235, f32[16384]{0:T(1024)S(1)} %bitcast.62, f32[16384]{0:T(1024)S(1)} %bitcast.61), kind=kLoop, calls=%fused_computation.10.clone.1 | loop fusion | flops 18874368 | bytes 25296896 | tf_op jit(solution)/shard_map/convert.4
  151.4 4.1 %fusion.65 = (f32[16,16384]{1,0:T(8,128)S(1)}, f32[16,16384]{1,0:T(8,128)S(1)}) fusion(s32[16384]{0:T(1024)S(1)} %bitcast.56), kind=kLoop, calls=%fused_computation.59.clone.1 | loop fusion | flops 3670016 | bytes 2162688 | tf_op jit(solution)/shard_map/while/body/eval_jaxpr/cos | solution.py:16
  155.4 4.2 %subtract_convert_fusion.2 = (bf16[8,16,16384]{2,1,0:T(8,128)(2,1)}, bf16[8,16,16384]{2,1,0:T(8,128)(2,1)}) fusion(f32[16,16384]{1,0:T(8,128)S(1)} %get-tuple-element.219, f32[8,16384]{1,0:T(8,128)S(1)} %get-tuple-element.225, f32[16,16384]{1,0:T(8,128)S(1)} %get-tuple-element.226, f32[8,16384]{1,0:T(8,128)S(1)} %get-tuple-element.227), kind=kLoop, calls=%fused_computation.17.clone.1 | loop fusion | flops 16777216 | bytes 11534336 | tf_op jit(solution)/shard_map/convert.3
  159.7 8.2 %fusion.69 = f32[128,128]{1,0:T(8,128)S(1)} fusion(bf16[128,16384]{1,0:T(8,128)(2,1)} %bitcast.53, bf16[128,16384]{1,0:T(8,128)(2,1)} %bitcast.52, bf16[128,16384]{1,0:T(8,128)(2,1)} %get-tuple-element.238, bf16[128,16384]{1,0:T(8,128)(2,1)} %get-tuple-element.239, f32[128,128]{1,0:T(8,128)S(1)} %get-tuple-element.252, pred[]{:T(512)S(6)} %compare.15), kind=kOutput, calls=%fused_computation.48.clone.1 | convolution fusion | flops 1107329024 | bytes 16908288 | tf_op jit(solution)/shard_map/while/body/eval_jaxpr/dot_general | solution.py:49
  167.9 0.6 copy-done
  168.5 26.3 %reduce-scatter.2.cloned.1.call-done = f32[32,128]{1,0:T(8,128)} async-done(((f32[128,128]{1,0:T(8,128)}), f32[32,128]{1,0:T(8,128)}) %reduce-scatter.2.cloned.1.call-update) | async-done | bytes 16400 | tf_op jit(solution)/shard_map/reduce_scatter | solution.py:86
  194.8 1.3 multiply_bitcast_fusion
  (14 shorter events, 2.4 us)
Async XLA Ops:
  6.5 188.3 %reduce-scatter.2.cloned.1.call-start = ((), (), s32[]{:S(2)}) async-start(), calls=%async_computation.1 | async-start | bytes 81920 | tf_op jit(solution)/shard_map/reduce_scatter | solution.py:86
  167.9 0.6 copy-start
Sparse Core Ops, SparseCore 0:
  168.7 26.1 reduce-scatter.1
where the time goes:
time: 203 us
  blocking collectives  88.1 us (43%)
  other arithmetic  55.2 us (27%)
  waiting for transfers between devices  26.3 us (13%)
  matrix products  16.4 us (8%)
  between operations  14.7 us (7%)
  local copies, waits for them, and re-layouts  2.13 us (1%)
    all_gather x1, blocking collectives, body(): lax.all_gather(packed, 'facet', axis=0, tiled=True)  88.1 us
    reduce_scatter x1, waiting for transfers between devices, body(): share = lax.psum_scatter(image, 'freq', scatter_dimension=0, tiled=True)  26.3 us
    another operation x4, other arithmetic  19.3 us
    cos x6, other arithmetic, angle_table(): return (jnp.cos(turns), jnp.sin(turns))  17.3 us
    dot_general x2, matrix products, facet_image(): lax.dot_general(left, right, (((1,), (1,)), ((), ())), preferred_element_...  16.4 us
    sub x2, other arithmetic, phase_table(): outer_cos = base_cos * coarse_cos - base_sin * coarse_sin  8.67 us
    sub x2, other arithmetic, phase_table(): outer_cos[:, None, :] * fine_cos[None, :, :]  4.64 us
  transfers between devices with their start and end apart: 1, of which 1 were waited for; matrix products, arithmetic and copies ran while one was open for 0% of the time, Pallas kernels for 0%

commit v1 on v0

--- a/solution.py
+++ b/solution.py
@@ -78,10 +78,17 @@
     gains = jnp.sum(beam[0][:, None] * matches, axis=0)
     facet_col = facets[0, 0]
     facet_row = facets[0, 1]
+    deliver_matrix = lambda page, mesh_ax: jnp.concatenate(
+        lax.all_to_all(
+            jnp.stack([page] * lax.axis_size(mesh_ax), axis=0),
+            axis_name=mesh_ax,
+            split_axis=0,
+            concat_axis=0,
+        ),
+        0,
+    )
     image = slab_image(
-        flatten_blocks(lax.all_gather(packed, "facet", axis=0, tiled=True), gains),
-        facet_col,
-        facet_row,
+        flatten_blocks(deliver_matrix(packed, mesh_ax="facet"), gains), facet_col, facet_row
     )
     share = lax.psum_scatter(image, "freq", scatter_dimension=0, tiled=True)
     scale = 2.0 / math.sqrt(total_blocks * weights.shape[1] * lax.axis_size("freq"))

time: 203 us -> 128 us (0.63)
  blocking collectives: 88.1 us -> 0 us
  starting transfers between devices: 0.01 us -> 11.2 us
  local copies, waits for them, and re-layouts: 2.13 us -> 4.64 us
    all_gather x1 -> x0, blocking collectives: 88.1 us -> none  [body(): lax.all_gather(packed, 'facet', axis=0, tiled=True)]
    reduce_scatter x1, waiting for transfers between devices: 26.3 us -> 14.6 us  [body(): share = lax.psum_scatter(image, 'freq', scatter_dimension=0, tiled=True)]
    all_to_all x0 -> x1, starting transfers between devices: none -> 11.2 us  [body(): lax.all_to_all(jnp.stack([page] * lax.axis_size(mesh_ax), axis=0), axis_n...]
    all_to_all x0 -> x1, waiting for transfers between devices: none -> 10.7 us  [body(): lax.all_to_all(jnp.stack([page] * lax.axis_size(mesh_ax), axis=0), axis_n...]
  transfers between devices with their start and end apart: 1 -> 2, of which waited for: 1 -> 2; matrix products, arithmetic and copies ran while one was open for 0% -> 2% of each run, Pallas kernels for 0% -> 0%
where the time goes in v1:
time: 128 us; the launch traced here: 127 us
  other arithmetic  54.8 us (43%)
  waiting for transfers between devices  25.2 us (20%)
  matrix products  16.4 us (13%)
  between operations  14.8 us (12%)
  starting transfers between devices  11.2 us (9%)
  local copies, waits for them, and re-layouts  4.64 us (4%)
    another operation x4, other arithmetic  19.3 us
    cos x6, other arithmetic, angle_table(): return (jnp.cos(turns), jnp.sin(turns))  17.3 us
    dot_general x2, matrix products, facet_image(): lax.dot_general(left, right, (((1,), (1,)), ((), ())), preferred_element_...  16.4 us
    reduce_scatter x1, waiting for transfers between devices, body(): share = lax.psum_scatter(image, 'freq', scatter_dimension=0, tiled=True)  14.6 us
    all_to_all x1, starting transfers between devices, body(): lax.all_to_all(jnp.stack([page] * lax.axis_size(mesh_ax), axis=0), axis_n...  11.2 us
    all_to_all x1, waiting for transfers between devices, body(): lax.all_to_all(jnp.stack([page] * lax.axis_size(mesh_ax), axis=0), axis_n...  10.7 us
    sub x2, other arithmetic, phase_table(): outer_cos = base_cos * coarse_cos - base_sin * coarse_sin  8.67 us
    sub x2, other arithmetic, phase_table(): outer_cos[:, None, :] * fine_cos[None, :, :]  4.64 us
  transfers between devices with their start and end apart: 2, of which 2 were waited for; matrix products, arithmetic and copies ran while one was open for 2% of the time, Pallas kernels for 0%

profile of v1, /device:TPU:1, one launch (start us, length us, event | category | flops | bytes accessed | tf_op | source)
XLA Modules:
  0.0 127.4 jit_solution(11489990757071709084)
XLA Ops:
  7.2 0.7 multiply_bitcast_fusion.1
  8.0 0.7 pad_maximum_fusion
  8.7 1.0 stack.2
  9.7 11.2 %all-to-all-start = ((f32[32,2,5,512]{3,1,2,0:T(2,128)}), f32[32,2,5,512]{3,1,2,0:T(2,128)S(1)}, u32[]{:S(2)}, u32[]{:S(2)}) async-start(f32[32,2,5,512]{3,1,2,0:T(2,128)} %stack.2), calls=%async_computation | async-start | bytes 1310720 | tf_op jit(solution)/shard_map/all_to_all | solution.py:82
  20.9 1.3 %fusion.55 = (s32[1,1]{1,0:T(1,128)}, s32[1,1]{1,0:T(1,128)}) fusion(s32[1,2]{1,0:T(1,128)} %param.15), kind=kLoop, calls=%fused_computation.98 | loop fusion | bytes 16 | tf_op jit(solution)/shard_map/slice | solution.py:80
  23.5 0.8 select_reduce_fusion
  24.3 10.7 %all-to-all-done = f32[32,2,5,512]{3,1,2,0:T(2,128)S(1)} async-done(((f32[32,2,5,512]{3,1,2,0:T(2,128)}), f32[32,2,5,512]{3,1,2,0:T(2,128)S(1)}, u32[]{:S(2)}, u32[]{:S(2)}) %all-to-all-start) | async-done | bytes 655392 | tf_op jit(solution)/shard_map/all_to_all | solution.py:82
  36.8 67.2 %while.14 = (s32[]{:T(128)}, f32[128,128]{1,0:T(8,128)S(1)}, f32[2,5,16384]{2,1,0:T(8,128)S(1)}, s32[]{:T(128)}, s32[]{:T(128)}, /*index=5*/s32[]{:T(128)}, s32[]{:T(128)}, s32[]{}, s32[]{}, s32[]{}, /*index=10*/s32[]{}) while((s32[]{:T(128)}, f32[128,128]{1,0:T(8,128)S(1)}, f32[2,5,16384]{2,1,0:T(8,128)S(1)}, s32[]{:T(128)}, ...), condition=%wide.region_2.3_spmd.clone, body=%wide.region_1.2_spmd.clone.sunk | while | flops 1168670720 | bytes 81461504 | solution.py:61
  37.8 4.3 %multiply_subtract_fusion.5 = (f32[8,16384]{1,0:T(8,128)S(1)}, f32[8,16384]{1,0:T(8,128)S(1)}, f32[8,16384]{1,0:T(8,128)S(1)}, f32[8,16384]{1,0:T(8,128)S(1)}) fusion(f32[16384]{0:T(1024)S(1)} %get-tuple-element.221, s32[16384]{0:T(1024)S(1)} %bitcast.62, s32[8]{0:T(128)S(1)} %iota_multiply_fusion.2, f32[16384]{0:T(1024)S(1)} %get-tuple-element.222, ...), kind=kLoop, calls=%fused_computation.62.clone.1 | loop fusion | flops 5242880 | bytes 2490400 | tf_op jit(solution)/shard_map/while/body/eval_jaxpr/sub | solution.py:26
  42.2 4.1 %fusion.67 = (f32[16,16384]{1,0:T(8,128)S(1)}, f32[16,16384]{1,0:T(8,128)S(1)}) fusion(s32[16384]{0:T(1024)S(1)} %bitcast.63), kind=kLoop, calls=%fused_computation.61.clone.1 | loop fusion | flops 3670016 | bytes 2162688 | tf_op jit(solution)/shard_map/while/body/eval_jaxpr/cos | solution.py:16
  46.2 2.3 %multiply_subtract_fusion.6 = (f32[8,16,16384]{2,1,0:T(8,128)S(1)}, f32[8,16,16384]{2,1,0:T(8,128)S(1)}) fusion(f32[16,16384]{1,0:T(8,128)S(1)} %get-tuple-element.230, f32[8,16384]{1,0:T(8,128)S(1)} %get-tuple-element.231, f32[16,16384]{1,0:T(8,128)S(1)} %get-tuple-element.232, f32[8,16384]{1,0:T(8,128)S(1)} %get-tuple-element.233), kind=kLoop, calls=%fused_computation.19.clone.1 | loop fusion | flops 12582912 | bytes 19922944 | tf_op jit(solution)/shard_map/while/body/eval_jaxpr/sub | solution.py:29
  48.6 5.4 %fusion.68 = (bf16[128,16384]{1,0:T(8,128)(2,1)}, bf16[128,16384]{1,0:T(8,128)(2,1)}) fusion(f32[8,16,16384]{2,1,0:T(8,128)S(1)} %get-tuple-element.234, f32[8,16,16384]{2,1,0:T(8,128)S(1)} %get-tuple-element.235, f32[16384]{0:T(1024)S(1)} %bitcast.66, f32[16384]{0:T(1024)S(1)} %bitcast.65), kind=kLoop, calls=%fused_computation.10.clone.1 | loop fusion | flops 18874368 | bytes 25296896 | tf_op jit(solution)/shard_map/convert.4
  54.0 4.1 %fusion.65 = (f32[16,16384]{1,0:T(8,128)S(1)}, f32[16,16384]{1,0:T(8,128)S(1)}) fusion(s32[16384]{0:T(1024)S(1)} %bitcast.60), kind=kLoop, calls=%fused_computation.59.clone.1 | loop fusion | flops 3670016 | bytes 2162688 | tf_op jit(solution)/shard_map/while/body/eval_jaxpr/cos | solution.py:16
  58.1 4.2 %subtract_convert_fusion.2 = (bf16[8,16,16384]{2,1,0:T(8,128)(2,1)}, bf16[8,16,16384]{2,1,0:T(8,128)(2,1)}) fusion(f32[16,16384]{1,0:T(8,128)S(1)} %get-tuple-element.219, f32[8,16384]{1,0:T(8,128)S(1)} %get-tuple-element.225, f32[16,16384]{1,0:T(8,128)S(1)} %get-tuple-element.226, f32[8,16384]{1,0:T(8,128)S(1)} %get-tuple-element.227), kind=kLoop, calls=%fused_computation.17.clone.1 | loop fusion | flops 16777216 | bytes 11534336 | tf_op jit(solution)/shard_map/convert.3
  62.3 8.2 %fusion.69 = f32[128,128]{1,0:T(8,128)S(1)} fusion(bf16[128,16384]{1,0:T(8,128)(2,1)} %bitcast.57, bf16[128,16384]{1,0:T(8,128)(2,1)} %bitcast.56, bf16[128,16384]{1,0:T(8,128)(2,1)} %get-tuple-element.238, bf16[128,16384]{1,0:T(8,128)(2,1)} %get-tuple-element.239, f32[128,128]{1,0:T(8,128)S(1)} %get-tuple-element.252, pred[]{:T(512)S(6)} %compare.15), kind=kOutput, calls=%fused_computation.48.clone.1 | convolution fusion | flops 1107329024 | bytes 16908288 | tf_op jit(solution)/shard_map/while/body/eval_jaxpr/dot_general | solution.py:49
  71.3 4.3 %multiply_subtract_fusion.5 = (f32[8,16384]{1,0:T(8,128)S(1)}, f32[8,16384]{1,0:T(8,128)S(1)}, f32[8,16384]{1,0:T(8,128)S(1)}, f32[8,16384]{1,0:T(8,128)S(1)}) fusion(f32[16384]{0:T(1024)S(1)} %get-tuple-element.221, s32[16384]{0:T(1024)S(1)} %bitcast.62, s32[8]{0:T(128)S(1)} %iota_multiply_fusion.2, f32[16384]{0:T(1024)S(1)} %get-tuple-element.222, ...), kind=kLoop, calls=%fused_computation.62.clone.1 | loop fusion | flops 5242880 | bytes 2490400 | tf_op jit(solution)/shard_map/while/body/eval_jaxpr/sub | solution.py:26
  75.7 4.1 %fusion.67 = (f32[16,16384]{1,0:T(8,128)S(1)}, f32[16,16384]{1,0:T(8,128)S(1)}) fusion(s32[16384]{0:T(1024)S(1)} %bitcast.63), kind=kLoop, calls=%fused_computation.61.clone.1 | loop fusion | flops 3670016 | bytes 2162688 | tf_op jit(solution)/shard_map/while/body/eval_jaxpr/cos | solution.py:16
  79.8 2.3 %multiply_subtract_fusion.6 = (f32[8,16,16384]{2,1,0:T(8,128)S(1)}, f32[8,16,16384]{2,1,0:T(8,128)S(1)}) fusion(f32[16,16384]{1,0:T(8,128)S(1)} %get-tuple-element.230, f32[8,16384]{1,0:T(8,128)S(1)} %get-tuple-element.231, f32[16,16384]{1,0:T(8,128)S(1)} %get-tuple-element.232, f32[8,16384]{1,0:T(8,128)S(1)} %get-tuple-element.233), kind=kLoop, calls=%fused_computation.19.clone.1 | loop fusion | flops 12582912 | bytes 19922944 | tf_op jit(solution)/shard_map/while/body/eval_jaxpr/sub | solution.py:29
  82.1 5.4 %fusion.68 = (bf16[128,16384]{1,0:T(8,128)(2,1)}, bf16[128,16384]{1,0:T(8,128)(2,1)}) fusion(f32[8,16,16384]{2,1,0:T(8,128)S(1)} %get-tuple-element.234, f32[8,16,16384]{2,1,0:T(8,128)S(1)} %get-tuple-element.235, f32[16384]{0:T(1024)S(1)} %bitcast.66, f32[16384]{0:T(1024)S(1)} %bitcast.65), kind=kLoop, calls=%fused_computation.10.clone.1 | loop fusion | flops 18874368 | bytes 25296896 | tf_op jit(solution)/shard_map/convert.4
  87.5 4.1 %fusion.65 = (f32[16,16384]{1,0:T(8,128)S(1)}, f32[16,16384]{1,0:T(8,128)S(1)}) fusion(s32[16384]{0:T(1024)S(1)} %bitcast.60), kind=kLoop, calls=%fused_computation.59.clone.1 | loop fusion | flops 3670016 | bytes 2162688 | tf_op jit(solution)/shard_map/while/body/eval_jaxpr/cos | solution.py:16
  91.6 4.2 %subtract_convert_fusion.2 = (bf16[8,16,16384]{2,1,0:T(8,128)(2,1)}, bf16[8,16,16384]{2,1,0:T(8,128)(2,1)}) fusion(f32[16,16384]{1,0:T(8,128)S(1)} %get-tuple-element.219, f32[8,16384]{1,0:T(8,128)S(1)} %get-tuple-element.225, f32[16,16384]{1,0:T(8,128)S(1)} %get-tuple-element.226, f32[8,16384]{1,0:T(8,128)S(1)} %get-tuple-element.227), kind=kLoop, calls=%fused_computation.17.clone.1 | loop fusion | flops 16777216 | bytes 11534336 | tf_op jit(solution)/shard_map/convert.3
  95.8 8.2 %fusion.69 = f32[128,128]{1,0:T(8,128)S(1)} fusion(bf16[128,16384]{1,0:T(8,128)(2,1)} %bitcast.57, bf16[128,16384]{1,0:T(8,128)(2,1)} %bitcast.56, bf16[128,16384]{1,0:T(8,128)(2,1)} %get-tuple-element.238, bf16[128,16384]{1,0:T(8,128)(2,1)} %get-tuple-element.239, f32[128,128]{1,0:T(8,128)S(1)} %get-tuple-element.252, pred[]{:T(512)S(6)} %compare.15), kind=kOutput, calls=%fused_computation.48.clone.1 | convolution fusion | flops 1107329024 | bytes 16908288 | tf_op jit(solution)/shard_map/while/body/eval_jaxpr/dot_general | solution.py:49
  104.7 14.6 %reduce-scatter.2.cloned.1.call-done = f32[32,128]{1,0:T(8,128)} async-done(((f32[128,128]{1,0:T(8,128)}), f32[32,128]{1,0:T(8,128)}) %reduce-scatter.2.cloned.1.call-update) | async-done | bytes 16400 | tf_op jit(solution)/shard_map/reduce_scatter | solution.py:93
  119.2 1.3 %multiply_bitcast_fusion = f32[1,32,128]{2,1,0:T(8,128)} fusion(f32[32,128]{1,0:T(8,128)} %reduce-scatter.2.cloned.1.call-done), kind=kLoop, calls=%fused_computation.95 | loop fusion | flops 4096 | bytes 32768 | tf_op jit(solution)/shard_map/broadcast_in_dim | solution.py:95
  (21 shorter events, 4.8 us)
Async XLA Ops:
  9.7 25.3 %all-to-all-start = ((f32[32,2,5,512]{3,1,2,0:T(2,128)}), f32[32,2,5,512]{3,1,2,0:T(2,128)S(1)}, u32[]{:S(2)}, u32[]{:S(2)}) async-start(f32[32,2,5,512]{3,1,2,0:T(2,128)} %stack.2), calls=%async_computation | async-start | bytes 1310720 | tf_op jit(solution)/shard_map/all_to_all | solution.py:82
  20.9 98.4 %reduce-scatter.2.cloned.1.call-start = ((), (), s32[]{:S(2)}) async-start(), calls=%async_computation.2 | async-start | bytes 81920 | tf_op jit(solution)/shard_map/reduce_scatter | solution.py:93
  104.0 0.6 copy-start
Sparse Core Ops, SparseCore 0:
  104.8 14.3 reduce-scatter.1
